TPU v7x, 32 devices: a whole 2x2x4 slice. The times are simulated.
32 devices in a mesh: dp: 4 (over y, core), fsdp: 8 (over z, x).
Axes of the slice: x: 2, y: 2, z: 4, core: 2. Of those that a mesh axis runs over, the one named last changes fastest.
Arguments:
- tokens: bfloat16 [32768, 768], P(('dp', 'fsdp')), may hold values from -6 to 6
- cotangent: bfloat16 [32768, 768], P(('dp', 'fsdp')), may hold values from -6 to 6
- segment_ids: int32 [64, 512], P(('dp', 'fsdp')), may hold values from 0 to 47, never falling along the last dimension, each value on 1 to 16 neighbouring positions
- w_attn: float32 [768, 2304], P('fsdp'), may hold values from -0.3125 to 0.3125
- moment_attn: float32 [768, 2304], P('fsdp'), may hold values from -543.058 to 543.058
- square_attn: float32 [768, 2304], P('fsdp'), may hold values from 3276.8 to 26214.4
- w_proj: float32 [768, 768], P('fsdp'), may hold values from -0.4375 to 0.4375
- moment_proj: float32 [768, 768], P('fsdp'), may hold values from -543.058 to 543.058
- square_proj: float32 [768, 768], P('fsdp'), may hold values from 3276.8 to 26214.4
- w_up: float32 [768, 3072], P('fsdp'), may hold values from -0.21875 to 0.21875
- moment_up: float32 [768, 3072], P('fsdp'), may hold values from -543.058 to 543.058
- square_up: float32 [768, 3072], P('fsdp'), may hold values from 3276.8 to 26214.4
- w_down: float32 [3072, 768], P('fsdp'), may hold values from -0.15625 to 0.15625
- moment_down: float32 [3072, 768], P('fsdp'), may hold values from -543.058 to 543.058
- square_down: float32 [3072, 768], P('fsdp'), may hold values from 3276.8 to 26214.4
- vectors: float32 [768, 12], P('fsdp'), may hold values from -1.2 to 1.3
- moment_vec: float32 [768, 12], P('fsdp'), may hold values from -905.0967 to 905.0967
- square_vec: float32 [768, 12], P('fsdp'), may hold values from 16384 to 131072
Outputs:
- block_out: bfloat16 [32768, 768], P(('dp', 'fsdp'))
- grad_tokens: float32 [32768, 768], P(('dp', 'fsdp'))
- attn_new: float32 [768, 2304], P('fsdp')
- attn_moment: float32 [768, 2304], P('fsdp')
- attn_square: float32 [768, 2304], P('fsdp')
- proj_new: float32 [768, 768], P('fsdp')
- proj_moment: float32 [768, 768], P('fsdp')
- proj_square: float32 [768, 768], P('fsdp')
- up_new: float32 [768, 3072], P('fsdp')
- up_moment: float32 [768, 3072], P('fsdp')
- up_square: float32 [768, 3072], P('fsdp')
- down_new: float32 [3072, 768], P('fsdp')
- down_moment: float32 [3072, 768], P('fsdp')
- down_square: float32 [3072, 768], P('fsdp')
- vec_new: float32 [768, 12], P('fsdp')
- vec_moment: float32 [768, 12], P('fsdp')
- vec_square: float32 [768, 12], P('fsdp')
Inputs may be any that keep to these rules, and one draw needn't show every extreme that they name: `segment_ids`: ids never fall along a block; each caption holds 1 to 16 rows, one of them exactly 16.
All inputs are finite; a program needn't handle non-finite values.
Results may differ from a plain program's by a relative error of at most 0.012.
The roundings to bfloat16 on the way count: a program that leaves them out, or rounds other values in their place, can miss the bound.
Values may be sent and summed in bfloat16 or wider, within the bound.
No kernel may reach another device: no remote copies, remote signals or barrier semaphores. Data moves between devices by JAX's collectives and lax.ppermute only.
A program may use at most 192 MiB of HBM per device.

v0:
```python
import jax
import jax.numpy as jnp
from jax import lax
from jax.sharding import PartitionSpec as P

D = 768
HEADS = 12
HEAD = 64
FF = 3072
PACK = 512
STEP = 5
eps_norm = 1e-06
beta_one = 0.5
beta_two = 0.5
rate_matrix = 0.03
rate_vector = 0.25
weight_decay = 0.1
eps_adam = 1e-08
masked_score = -1e30


def layer_norm(rows_in, gain_vec, shift_vec):
    row_mean = jnp.mean(rows_in, axis=-1, keepdims=True)
    centered = rows_in - row_mean
    row_var = jnp.mean(centered * centered, axis=-1, keepdims=True)
    return centered * lax.rsqrt(row_var + eps_norm) * gain_vec + shift_vec


def contract_rows(left, right):
    return lax.dot_general(
        left, right, (((0,), (0,)), ((), ())), preferred_element_type=jnp.float32
    )


def contract_cols(left, right):
    return lax.dot_general(
        left, right, (((1,), (1,)), ((), ())), preferred_element_type=jnp.float32
    )


def scores_of(qkv_pack, seg_pack):
    queries = qkv_pack[:, :D].reshape(PACK, HEADS, HEAD)
    key_rows = qkv_pack[:, D : 2 * D].reshape(PACK, HEADS, HEAD)
    values = qkv_pack[:, 2 * D :].reshape(PACK, HEADS, HEAD)
    scores = jnp.einsum(
        "qhd,khd->hqk", queries, key_rows, preferred_element_type=jnp.float32
    ) * HEAD ** (-0.5)
    same_caption = seg_pack[:, None] == seg_pack[None, :]
    scores = jnp.where(same_caption[None], scores, masked_score)
    return (queries, key_rows, values, scores)


def attend(packed):
    qkv_pack, seg_pack = packed
    queries, key_rows, values, scores = scores_of(qkv_pack, seg_pack)
    row_max = jnp.max(scores, axis=-1, keepdims=True)
    exp_scores = jnp.exp(scores - row_max)
    exp_total = jnp.sum(exp_scores, axis=-1, keepdims=True)
    soft_weights = (exp_scores / exp_total).astype(jnp.bfloat16)
    mixed_pack = jnp.einsum(
        "hqk,khd->qhd", soft_weights, values, preferred_element_type=jnp.float32
    )
    return (
        mixed_pack.reshape(PACK, D).astype(jnp.bfloat16),
        (row_max + jnp.log(exp_total))[..., 0],
    )


def attend_back(packed):
    qkv_pack, seg_pack, log_total, grad_pack = packed
    queries, key_rows, values, scores = scores_of(qkv_pack, seg_pack)
    soft_exact = jnp.exp(scores - log_total[..., None])
    grad_heads = grad_pack.reshape(PACK, HEADS, HEAD)
    grad_soft = jnp.einsum("qhd,khd->hqk", grad_heads, values, preferred_element_type=jnp.float32)
    row_delta = jnp.sum(soft_exact * grad_soft, axis=-1, keepdims=True)
    grad_score = (soft_exact * (grad_soft - row_delta)).astype(jnp.bfloat16)
    score_scale = HEAD ** (-0.5)
    grad_queries = (
        jnp.einsum("hqk,khd->qhd", grad_score, key_rows, preferred_element_type=jnp.float32)
        * score_scale
    )
    grad_keys = (
        jnp.einsum("hqk,qhd->khd", grad_score, queries, preferred_element_type=jnp.float32)
        * score_scale
    )
    grad_values = jnp.einsum(
        "hqk,qhd->khd",
        soft_exact.astype(jnp.bfloat16),
        grad_heads,
        preferred_element_type=jnp.float32,
    )
    joined = jnp.concatenate(
        [grad_queries.reshape(PACK, D), grad_keys.reshape(PACK, D), grad_values.reshape(PACK, D)],
        axis=1,
    )
    return joined.astype(jnp.bfloat16)


def adam_step(master, moment, square, gradient, rate, decay_rate):
    moment_new = beta_one * moment + (1.0 - beta_one) * gradient
    square_new = beta_two * square + (1.0 - beta_two) * gradient * gradient
    moment_hat = moment_new / (1.0 - beta_one**STEP)
    square_hat = square_new / (1.0 - beta_two**STEP)
    master_new = master - rate * (
        moment_hat / (jnp.sqrt(square_hat) + eps_adam) + decay_rate * master
    )
    return (master_new, moment_new, square_new)


def body(
    tokens,
    cotangent,
    segment_ids,
    w_attn,
    moment_attn,
    square_attn,
    w_proj,
    moment_proj,
    square_proj,
    w_up,
    moment_up,
    square_up,
    w_down,
    moment_down,
    square_down,
    vectors,
    moment_vec,
    square_vec,
):
    low_attn = w_attn.astype(jnp.bfloat16)
    low_proj = w_proj.astype(jnp.bfloat16)
    low_up = w_up.astype(jnp.bfloat16)
    low_down = w_down.astype(jnp.bfloat16)
    low_vec = vectors.astype(jnp.bfloat16)
    full_attn, full_proj, full_up, full_down, full_vec = (
        lax.all_gather(low_attn, "fsdp", axis=0, tiled=True),
        lax.all_gather(low_proj, "fsdp", axis=0, tiled=True),
        lax.all_gather(low_up, "fsdp", axis=0, tiled=True),
        lax.all_gather(low_down, "fsdp", axis=0, tiled=True),
        lax.all_gather(low_vec, "fsdp", axis=0, tiled=True),
    )
    vec_full = full_vec.astype(jnp.float32)
    gain_one = vec_full[:, 0]
    shift_one = vec_full[:, 1]
    q_bias = vec_full[:, 2]
    v_bias = vec_full[:, 3]
    out_bias = vec_full[:, 4]
    gain_two = vec_full[:, 5]
    shift_two = vec_full[:, 6]
    down_bias = vec_full[:, 7]
    up_bias = vec_full[:, 8:12].T.reshape(FF)
    row_count = tokens.shape[0]
    pack_count = row_count // PACK
    inputs = tokens.astype(jnp.float32)
    normed_one = layer_norm(inputs, gain_one, shift_one).astype(jnp.bfloat16)
    qkv_bias = jnp.concatenate([q_bias, jnp.zeros_like(q_bias), v_bias])
    qkv = (jnp.dot(normed_one, full_attn, preferred_element_type=jnp.float32) + qkv_bias).astype(
        jnp.bfloat16
    )
    qkv_packs = qkv.reshape(pack_count, PACK, 3 * D)
    mixed_rows, log_total = lax.map(attend, (qkv_packs, segment_ids))
    mixed_rows = mixed_rows.reshape(row_count, D)
    residual = (
        inputs + jnp.dot(mixed_rows, full_proj, preferred_element_type=jnp.float32) + out_bias
    )
    normed_two = layer_norm(residual, gain_two, shift_two).astype(jnp.bfloat16)
    pre_act = jnp.dot(normed_two, full_up, preferred_element_type=jnp.float32) + up_bias
    activated = jax.nn.gelu(pre_act).astype(jnp.bfloat16)
    output = (
        residual + jnp.dot(activated, full_down, preferred_element_type=jnp.float32) + down_bias
    )
    back_attn, back_proj, back_up, back_down = (
        lax.all_gather(low_attn, "fsdp", axis=0, tiled=True),
        lax.all_gather(low_proj, "fsdp", axis=0, tiled=True),
        lax.all_gather(low_up, "fsdp", axis=0, tiled=True),
        lax.all_gather(low_down, "fsdp", axis=0, tiled=True),
    )
    grad_rows = cotangent.astype(jnp.float32)
    grad_down = contract_rows(activated, cotangent)
    grad_down_bias = jnp.sum(grad_rows, axis=0)
    grad_act = contract_cols(cotangent, back_down)
    gelu_value, gelu_pull = jax.vjp(jax.nn.gelu, pre_act)
    grad_pre = gelu_pull(grad_act)[0].astype(jnp.bfloat16)
    grad_up = contract_rows(normed_two, grad_pre)
    grad_up_bias = jnp.sum(grad_pre.astype(jnp.float32), axis=0)
    grad_normed_two = contract_cols(grad_pre, back_up)
    norm_value, second_pull = jax.vjp(layer_norm, residual, gain_two, shift_two)
    grad_resid_part, grad_gain_two, grad_shift_two = second_pull(grad_normed_two)
    grad_resid = grad_rows + grad_resid_part
    sum_up, sum_down = (
        lax.psum_scatter(grad_up, "fsdp", scatter_dimension=0, tiled=True),
        lax.psum_scatter(grad_down, "fsdp", scatter_dimension=0, tiled=True),
    )
    grad_branch = grad_resid.astype(jnp.bfloat16)
    grad_proj = contract_rows(mixed_rows, grad_branch)
    grad_out_bias = jnp.sum(grad_branch.astype(jnp.float32), axis=0)
    grad_mixed = contract_cols(grad_branch, back_proj).astype(jnp.bfloat16)
    grad_qkv = lax.map(
        attend_back, (qkv_packs, segment_ids, log_total, grad_mixed.reshape(pack_count, PACK, D))
    )
    grad_qkv = grad_qkv.reshape(row_count, 3 * D)
    grad_attn = contract_rows(normed_one, grad_qkv)
    qkv_bias_grad = jnp.sum(grad_qkv.astype(jnp.float32), axis=0)
    grad_normed_one = contract_cols(grad_qkv, back_attn)
    first_value, first_pull = jax.vjp(layer_norm, inputs, gain_one, shift_one)
    grad_in_part, grad_gain_one, grad_shift_one = first_pull(grad_normed_one)
    grad_inputs = grad_resid + grad_in_part
    grad_columns = jnp.stack(
        [
            grad_gain_one,
            grad_shift_one,
            qkv_bias_grad[:D],
            qkv_bias_grad[2 * D :],
            grad_out_bias,
            grad_gain_two,
            grad_shift_two,
            grad_down_bias,
        ],
        axis=1,
    )
    grad_vec = jnp.concatenate([grad_columns, grad_up_bias.reshape(4, D).T], axis=1)
    sum_attn, sum_proj, sum_vec = (
        lax.psum_scatter(grad_attn, "fsdp", scatter_dimension=0, tiled=True),
        lax.psum_scatter(grad_proj, "fsdp", scatter_dimension=0, tiled=True),
        lax.psum_scatter(grad_vec, "fsdp", scatter_dimension=0, tiled=True),
    )
    total_attn, total_proj, total_up, total_down, total_vec = lax.psum(
        (sum_attn, sum_proj, sum_up, sum_down, sum_vec), "dp"
    )
    attn_upd = adam_step(w_attn, moment_attn, square_attn, total_attn, rate_matrix, weight_decay)
    proj_upd = adam_step(w_proj, moment_proj, square_proj, total_proj, rate_matrix, weight_decay)
    up_upd = adam_step(w_up, moment_up, square_up, total_up, rate_matrix, weight_decay)
    down_upd = adam_step(w_down, moment_down, square_down, total_down, rate_matrix, weight_decay)
    vec_upd = adam_step(vectors, moment_vec, square_vec, total_vec, rate_vector, 0.0)
    return (
        output.astype(jnp.bfloat16),
        grad_inputs,
        attn_upd[0],
        attn_upd[1],
        attn_upd[2],
        proj_upd[0],
        proj_upd[1],
        proj_upd[2],
        up_upd[0],
        up_upd[1],
        up_upd[2],
        down_upd[0],
        down_upd[1],
        down_upd[2],
        vec_upd[0],
        vec_upd[1],
        vec_upd[2],
    )


def solution(mesh):
    in_specs = (
        P(("dp", "fsdp"), None),
        P(("dp", "fsdp"), None),
        P(("dp", "fsdp"), None),
        P("fsdp", None),
        P("fsdp", None),
        P("fsdp", None),
        P("fsdp", None),
        P("fsdp", None),
        P("fsdp", None),
        P("fsdp", None),
        P("fsdp", None),
        P("fsdp", None),
        P("fsdp", None),
        P("fsdp", None),
        P("fsdp", None),
        P("fsdp", None),
        P("fsdp", None),
        P("fsdp", None),
    )
    out_specs = (
        P(("dp", "fsdp"), None),
        P(("dp", "fsdp"), None),
        P("fsdp", None),
        P("fsdp", None),
        P("fsdp", None),
        P("fsdp", None),
        P("fsdp", None),
        P("fsdp", None),
        P("fsdp", None),
        P("fsdp", None),
        P("fsdp", None),
        P("fsdp", None),
        P("fsdp", None),
        P("fsdp", None),
        P("fsdp", None),
        P("fsdp", None),
        P("fsdp", None),
    )
    return jax.shard_map(body, mesh=mesh, in_specs=in_specs, out_specs=out_specs, check_vma=False)
```

profile of v0, /device:TPU:0, one launch (start us, length us, event | category | flops | bytes accessed | tf_op | source)
XLA Modules:
  0.0 1021.2 jit_solution(2336385018633477261)
XLA Ops:
  13.1 33.0 %all-gather = bf16[8,96,12]{1,2,0:T(8,128)(2,1)S(1)} all-gather(bf16[1,96,12]{1,2,0:T(8,128)(2,1)S(1)} %convert_bitcast_fusion), channel_id=1, replica_groups=mesh['dp'=4,'fsdp'=8] {'fsdp'}, dimensions={0}, use_global_device_ids=true | all-gather | bytes 20736 | tf_op jit(solution)/shard_map/all_gather | solution.py:140
  52.6 25.7 %all-gather.6.cloned.1.call-done = bf16[768,2304]{1,0:T(8,128)(2,1)} async-done(((bf16[96,2304]{1,0:T(8,128)(2,1)}), bf16[768,2304]{1,0:T(8,128)(2,1)}) %all-gather.6.cloned.1.call-update) | async-done | bytes 3538960 | tf_op jit(solution)/shard_map/all_gather | solution.py:136
  78.3 7.7 add_convert_fusion
  92.8 27.6 %while.22 = (s32[]{:T(128)}, bf16[2,512,768]{2,1,0:T(8,128)(2,1)}, f32[2,12,512]{2,1,0:T(8,128)S(1)}, bf16[2,512,2304]{1,2,0:T(8,128)(2,1)}, s32[2,512]{1,0:T(2,128)S(1)}, /*index=5*/s32[]{:T(128)}) while((s32[]{:T(128)}, bf16[2,512,768]{2,1,0:T(8,128)(2,1)}, f32[2,12,512]{2,1,0:T(8,128)S(1)}, bf16[2,512,2304]{1,2,0:T(8,128)(2,1)}, ...), condition=%wide.region_5.6_spmd, body=%wide.region_2.5_spmd.sunk | while | flops 843704320 | bytes 54753372 | solution.py:161
  128.3 73.5 %all-gather.10.cloned.1.call-done = bf16[768,3072]{1,0:T(8,128)(2,1)} async-done(((bf16[96,3072]{1,0:T(8,128)(2,1)}), bf16[768,3072]{1,0:T(8,128)(2,1)}) %all-gather.10.cloned.1.call-update) | async-done | bytes 4718608 | tf_op jit(solution)/shard_map/all_gather | solution.py:138
  201.8 11.2 %fusion.47 = f32[1024,3072]{1,0:T(8,128)} fusion(bf16[768,3072]{1,0:T(8,128)(2,1)} %all-gather.10.cloned.1.call-done, f32[1024,768]{0,1:T(8,128)} %get-tuple-element.264, f32[768]{0:T(1024)S(1)} %copy-done.28, f32[768]{0:T(1024)S(1)} %copy-done.24, f32[1024]{0:T(1024)S(1)} %fusion.42, f32[1024]{0:T(1024)S(1)} %broadcast_multiply_fusion), kind=kOutput, calls=%fused_computation.117 | convolution fusion | flops 4835770368 | bytes 20461568 | tf_op jit(solution)/shard_map/dot_general | solution.py:167
  213.0 69.1 %all-gather.12.cloned.1.call-done = bf16[3072,768]{1,0:T(8,128)(2,1)} async-done(((bf16[384,768]{1,0:T(8,128)(2,1)}), bf16[3072,768]{1,0:T(8,128)(2,1)}) %all-gather.12.cloned.1.call-update) | async-done | bytes 4718608 | tf_op jit(solution)/shard_map/all_gather | solution.py:139
  282.1 15.5 %convert_reduce_fusion = (f32[3072]{0:T(1024)}, bf16[1024,3072]{1,0:T(8,128)(2,1)S(1)}) fusion(f32[1024,3072]{1,0:T(8,128)} %fusion.47, f32[3072]{0:T(1024)S(1)} %copy-done.45, bf16[1024,768]{1,0:T(8,128)(2,1)S(1)} %copy-done.13, bf16[3072,768]{1,0:T(8,128)(2,1)} %all-gather.12.cloned.1.call-done), kind=kOutput, calls=%fused_computation.40 | convolution fusion | flops 4904186880 | bytes 25190400 | tf_op jit(solution)/shard_map/dot_general | solution.py:36
  297.6 7.3 fusion.61
  304.9 13.8 %copy.99 = f32[1024,768]{0,1:T(8,128)S(1)} copy(f32[1024,768]{1,0:T(8,128)} %get-tuple-element.268) | data formatting | bytes 6291456 | tf_op jit(solution)/shard_map/dot_general | solution.py:36
  333.2 52.4 %while.23 = (s32[]{:T(128)}, bf16[2,512,2304]{1,2,0:T(8,128)(2,1)}, bf16[2,512,2304]{1,2,0:T(8,128)(2,1)}, s32[2,512]{1,0:T(2,128)S(1)}, f32[2,12,512]{2,1,0:T(8...) while((s32[]{:T(128)}, bf16[2,512,2304]{1,2,0:T(8,128)(2,1)}, bf16[2,512,2304]{1,2,0:T(8,128)(2,1)}, ...), condition=%wide.region_12.13_spmd, body=%wide.region_10.12_spmd.sunk | while | flops 2069751808 | bytes 120764512 | solution.py:198
  347.6 7.1 multiply_convert_fusion.9
  373.8 7.0 multiply_convert_fusion.9
  385.6 6.9 copy.102
  392.5 8.7 fusion.43
  402.6 13.0 %fusion.48 = f32[3072,768]{1,0:T(8,128)} fusion(bf16[1024,768]{1,0:T(8,128)(2,1)S(1)} %copy-done.14, f32[1024,3072]{1,0:T(8,128)} %fusion.47, f32[3072]{0:T(1024)S(1)} %copy-done.46), kind=kOutput, calls=%fused_computation.118 | convolution fusion | flops 4863295488 | bytes 23605248 | tf_op jit(solution)/shard_map/dot_general | solution.py:30
  416.3 10.6 %fusion.46 = f32[768,3072]{1,0:T(8,128)} fusion(bf16[1024,3072]{1,0:T(8,128)(2,1)} %copy-done.57, f32[1024,768]{0,1:T(8,128)} %get-tuple-element.264, f32[768]{0:T(1024)S(1)} %copy-done.29, f32[768]{0:T(1024)S(1)} %copy-done.25, f32[1024]{0:T(1024)S(1)} %copy-done.27, f32[1024]{0:T(1024)S(1)} %copy-done.23), kind=kOutput, calls=%fused_computation.116 | convolution fusion | flops 4835770368 | bytes 18888704 | tf_op jit(solution)/shard_map/dot_general | solution.py:30
  431.1 7.9 fusion.60
  452.4 78.3 %reduce-scatter.8.cloned.1.call-done = f32[96,2304]{1,0:T(8,128)} async-done(((f32[768,2304]{1,0:T(8,128)}), f32[96,2304]{1,0:T(8,128)}) %reduce-scatter.8.cloned.1.call-update) | async-done | bytes 884752 | tf_op jit(solution)/shard_map/reduce_scatter | solution.py:223
  530.7 164.9 %reduce-scatter.14.cloned.1.call-done = f32[384,768]{1,0:T(8,128)} async-done(((f32[3072,768]{1,0:T(8,128)}), f32[384,768]{1,0:T(8,128)}) %reduce-scatter.14.cloned.1.call-update) | async-done | bytes 1179664 | tf_op jit(solution)/shard_map/reduce_scatter | solution.py:192
  695.5 164.8 %reduce-scatter.12.cloned.1.call-done = f32[96,3072]{1,0:T(8,128)} async-done(((f32[768,3072]{1,0:T(8,128)}), f32[96,3072]{1,0:T(8,128)}) %reduce-scatter.12.cloned.1.call-update) | async-done | bytes 1179664 | tf_op jit(solution)/shard_map/reduce_scatter | solution.py:191
  860.4 12.3 %add_convert_fusion.1 = bf16[1024,768]{0,1:T(8,128)(2,1)} fusion(f32[1024,768]{0,1:T(8,128)} %get-tuple-element.264, bf16[3072,768]{1,0:T(8,128)(2,1)} %all-gather.12.cloned.1.call-done, f32[768]{0:T(1024)S(1)} %copy-done.50, f32[1024,3072]{1,0:T(8,128)} %fusion.47, f32[3072]{0:T(1024)S(1)} %copy-done.46), kind=kOutput, calls=%fused_computation.67 | convolution fusion | flops 4865654784 | bytes 22035456 | tf_op jit(solution)/shard_map/dot_general | solution.py:170
  877.8 47.6 %reduce-scatter.16.cloned.1.call-done = f32[96,12]{1,0:T(8,128)} async-done(((f32[768,12]{1,0:T(8,128)}), f32[96,12]{1,0:T(8,128)}) %reduce-scatter.16.cloned.1.call-update) | async-done | bytes 4624
  932.9 69.0 %all-reduce.3.cloned.1.call-done = (f32[96,2304]{1,0:T(8,128)}, f32[96,768]{1,0:T(8,128)}, f32[96,3072]{1,0:T(8,128)}, f32[384,768]{1,0:T(8,128)}) async-done(((f32[96,2304]{1,0:T(8,128)}, f32[96,768]{1,0:T(8,128)}, f32[96,3072]{1,0:T(8,128)}, f32[384,768]{1,0:T(8,128)}), (f32[96,2304]{1,0:T(8,128)}, f32[96,768]{1,0:T(8,128)}, f32[96,3072]{1,0:T(8,128)}, f32[384,768]{1,0:T(8,128)})) %all-reduce.3.cloned.1.call-update) | async-done | bytes 3538960 | tf_op jit(solution)/shard_map/psum | solution.py:227
  (245 shorter events, 150.9 us)
Async XLA Ops:
  7.2 71.1 %all-gather.6.cloned.1.call-start = ((), (), s32[]{:S(2)}) async-start(), calls=%async_computation.5 | async-start | bytes 3981312 | tf_op jit(solution)/shard_map/all_gather | solution.py:136
  9.4 111.6 %all-gather.8.cloned.1.call-start = ((), (), s32[]{:S(2)}) async-start(), calls=%async_computation.6 | async-start | bytes 1327104 | tf_op jit(solution)/shard_map/all_gather | solution.py:137
  11.1 190.7 %all-gather.10.cloned.1.call-start = ((), (), s32[]{:S(2)}) async-start(), calls=%async_computation.7 | async-start | bytes 5308416 | tf_op jit(solution)/shard_map/all_gather | solution.py:138
  12.1 270.0 %all-gather.12.cloned.1.call-start = ((), (), s32[]{:S(2)}) async-start(), calls=%async_computation.8 | async-start | bytes 5308416 | tf_op jit(solution)/shard_map/all_gather | solution.py:139
  13.1 439.3 %reduce-scatter.10.cloned.1.call-start = ((), (), s32[]{:S(2)}) async-start(), calls=%async_computation.10 | async-start | bytes 2654208 | tf_op jit(solution)/shard_map/reduce_scatter | solution.py:224
  49.2 71.8 %copy-start = (bf16[1024,768]{0,1:T(8,128)(2,1)}, bf16[1024,768]{0,1:T(8,128)(2,1)S(1)}, u32[]{:S(2)}) copy-start(bf16[1024,768]{0,1:T(8,128)(2,1)S(1)} %copy.93) | copy-start | bytes 4718596
  49.5 36.6 %copy-start.30 = (f32[1024]{0:T(1024)}, f32[1024]{0:T(1024)S(1)}, u32[]{:S(2)}) copy-start(f32[1024]{0:T(1024)S(1)} %broadcast_multiply_fusion.1) | copy-start | bytes 12292
  50.0 36.1 %copy-start.39 = (f32[1024]{0:T(1024)}, f32[1024]{0:T(1024)S(1)}, u32[]{:S(2)}) copy-start(f32[1024]{0:T(1024)S(1)} %fusion.31) | copy-start | bytes 12292
  126.0 75.8 %copy-start.24 = (f32[768]{0:T(1024)S(1)}, f32[768]{0:T(1024)}, u32[]{:S(2)}) copy-start(f32[768]{0:T(1024)} %get-tuple-element.196) | copy-start | bytes 9220
  126.0 75.8 %copy-start.28 = (f32[768]{0:T(1024)S(1)}, f32[768]{0:T(1024)}, u32[]{:S(2)}) copy-start(f32[768]{0:T(1024)} %get-tuple-element.198) | copy-start | bytes 9220
  126.0 196.1 %copy-start.22 = (f32[1024]{0:T(1024)}, f32[1024]{0:T(1024)S(1)}, u32[]{:S(2)}) copy-start(f32[1024]{0:T(1024)S(1)} %broadcast_multiply_fusion) | copy-start | bytes 12292
  128.2 193.9 %copy-start.26 = (f32[1024]{0:T(1024)}, f32[1024]{0:T(1024)S(1)}, u32[]{:S(2)}) copy-start(f32[1024]{0:T(1024)S(1)} %fusion.42) | copy-start | bytes 12292
  201.8 80.3 %copy-start.13 = (bf16[1024,768]{1,0:T(8,128)(2,1)S(1)}, bf16[1024,768]{1,0:T(8,128)(2,1)}, u32[]{:S(2)}) copy-start(bf16[1024,768]{1,0:T(8,128)(2,1)} %param.23) | copy-start | bytes 4718596
  201.8 80.3 %copy-start.45 = (f32[3072]{0:T(1024)S(1)}, f32[3072]{0:T(1024)}, u32[]{:S(2)}) copy-start(f32[3072]{0:T(1024)} %add.231) | copy-start | bytes 36868
  330.4 200.3 %reduce-scatter.8.cloned.1.call-start = ((), (), s32[]{:S(2)}) async-start(), calls=%async_computation.9 | async-start | bytes 7962624 | tf_op jit(solution)/shard_map/reduce_scatter | solution.py:223
  401.2 294.3 %reduce-scatter.14.cloned.1.call-start = ((), (), s32[]{:S(2)}) async-start(), calls=%async_computation.12 | async-start | bytes 10616832 | tf_op jit(solution)/shard_map/reduce_scatter | solution.py:192
  415.6 444.7 %reduce-scatter.12.cloned.1.call-start = ((), (), s32[]{:S(2)}) async-start(), calls=%async_computation.11 | async-start | bytes 10616832 | tf_op jit(solution)/shard_map/reduce_scatter | solution.py:191
  426.9 498.5 %reduce-scatter.16.cloned.1.call-start = ((), (), s32[]{:S(2)}) async-start(), calls=%async_computation.13 | async-start | bytes 442368
  451.3 409.1 %copy-start.50 = (f32[768]{0:T(1024)S(1)}, f32[768]{0:T(1024)}, u32[]{:S(2)}) copy-start(f32[768]{0:T(1024)} %get-tuple-element.197) | copy-start | bytes 9220
  452.3 549.6 %all-reduce.3.cloned.1.call-start = ((), (), s32[]{:S(2)}) async-start(), calls=%async_computation.14 | async-start | bytes 7077888 | tf_op jit(solution)/shard_map/psum | solution.py:227
  875.4 56.8 %copy-start.42 = (f32[96,12]{0,1:T(8,128)S(1)}, f32[96,12]{0,1:T(8,128)}, u32[]{:S(2)}) copy-start(f32[96,12]{0,1:T(8,128)} %param.37) | copy-start | bytes 13828
  875.4 56.8 %copy-start.48 = (f32[96,12]{0,1:T(8,128)S(1)}, f32[96,12]{0,1:T(8,128)}, u32[]{:S(2)}) copy-start(f32[96,12]{0,1:T(8,128)} %param.38) | copy-start | bytes 13828
  875.4 56.8 %copy-start.49 = (f32[96,12]{0,1:T(8,128)S(1)}, f32[96,12]{0,1:T(8,128)}, u32[]{:S(2)}) copy-start(f32[96,12]{0,1:T(8,128)} %param.39) | copy-start | bytes 13828
  875.4 126.4 %copy-start.15 = (f32[96,768]{1,0:T(8,128)S(1)}, f32[96,768]{1,0:T(8,128)}, u32[]{:S(2)}) copy-start(f32[96,768]{1,0:T(8,128)} %param.28) | copy-start | bytes 884740
  (44 other events, 267.8 us)
Sparse Core Ops, SparseCore 0:
  10.8 67.4 all-gather.5
  81.1 39.8 all-gather.7
  123.7 77.9 all-gather.9
  204.4 77.6 all-gather.11
  330.5 68.1 reduce-scatter.9
  402.3 128.3 reduce-scatter.7
  534.3 161.2 reduce-scatter.13
  699.1 161.1 reduce-scatter.11
  864.2 61.1 reduce-scatter.15
  927.9 73.9 all-reduce.2
where the time goes:
time: 1030 us; the launch traced here: 1020 us
  waiting for transfers between devices  694 us (67%)
  matrix products  147 us (14%)
  local copies, waits for them, and re-layouts  64 us (6%)
  other arithmetic  61.3 us (6%)
  blocking collectives  38.9 us (4%)
  between operations  14.9 us (1%)
    reduce_scatter x1, waiting for transfers between devices, body(): lax.psum_scatter(grad_down, 'fsdp', scatter_dimension=0, tiled=True)  165 us
    reduce_scatter x1, waiting for transfers between devices, body(): lax.psum_scatter(grad_up, 'fsdp', scatter_dimension=0, tiled=True)  165 us
    reduce_scatter x1, waiting for transfers between devices, body(): lax.psum_scatter(grad_attn, 'fsdp', scatter_dimension=0, tiled=True)  78.3 us
    all_gather x1, waiting for transfers between devices, body(): lax.all_gather(low_up, 'fsdp', axis=0, tiled=True)  73.5 us
    all_gather x1, waiting for transfers between devices, body(): lax.all_gather(low_down, 'fsdp', axis=0, tiled=True)  69.1 us
    psum x1, waiting for transfers between devices, body(): lax.psum((sum_attn, sum_proj, sum_up, sum_down, sum_vec), 'dp')  69 us
    unnamed x11, waiting for transfers between devices  47.8 us
    dot_general x4, matrix products, contract_rows(): lax.dot_general(left, right, (((0,), (0,)), ((), ())), preferred_element_...  35.1 us
  transfers between devices with their start and end apart: 10, of which 9 were waited for; matrix products, arithmetic and copies ran while one was open for 20% of the time, Pallas kernels for 0%

commit v1 on v0

--- a/solution.py
+++ b/solution.py
@@ -17,6 +17,22 @@
 weight_decay = 0.1
 eps_adam = 1e-08
 masked_score = -1e30
+
+
+def gather_around(x, axis, dim):
+    ways, here, step = (lax.axis_size(axis), lax.axis_index(axis), x.shape[dim])
+    shape = [n * ways if d == dim else n for d, n in enumerate(x.shape)]
+    full = lax.dynamic_update_slice_in_dim(jnp.zeros(shape, x.dtype), x, here * step, axis=dim)
+    going_up = going_down = x
+    for far in range(1, ways // 2 + 1):
+        going_up = lax.ppermute(going_up, axis, [(d, (d + 1) % ways) for d in range(ways)])
+        full = lax.dynamic_update_slice_in_dim(full, going_up, (here - far) % ways * step, axis=dim)
+        if 2 * far < ways:
+            going_down = lax.ppermute(going_down, axis, [(d, (d - 1) % ways) for d in range(ways)])
+            full = lax.dynamic_update_slice_in_dim(
+                full, going_down, (here + far) % ways * step, axis=dim
+            )
+    return full
 
 
 def layer_norm(rows_in, gain_vec, shift_vec):
@@ -137,7 +153,7 @@
         lax.all_gather(low_proj, "fsdp", axis=0, tiled=True),
         lax.all_gather(low_up, "fsdp", axis=0, tiled=True),
         lax.all_gather(low_down, "fsdp", axis=0, tiled=True),
-        lax.all_gather(low_vec, "fsdp", axis=0, tiled=True),
+        gather_around(low_vec, "fsdp", 0),
     )
     vec_full = full_vec.astype(jnp.float32)
     gain_one = vec_full[:, 0]

time: 1030 us -> 1030 us (level)
  blocking collectives: 38.9 us -> 5.75 us
  waiting for transfers between devices: 694 us -> 721 us
  starting transfers between devices: 0.42 us -> 16 us
    all_gather x1 -> x0, blocking collectives: 33 us -> none  [body(): lax.all_gather(low_vec, 'fsdp', axis=0, tiled=True)]
    ppermute x0 -> x7, starting transfers between devices: none -> 15.6 us  [the longest x3 15.6 us: gather_around(): lax.ppermute(going_down, axis, [(d, (d - 1) % ways) for d in range(ways)])]
    unnamed x11, waiting for transfers between devices: 47.8 us -> 59.9 us
    dot_general x2, local copies, waits for them, and re-layouts: 17.8 us -> 7.35 us  [contract_cols(): lax.dot_general(left, right, (((1,), (1,)), ((), ())), preferred_element_...]
  transfers between devices with their start and end apart: 10 -> 17, of which waited for: 9 -> 13; matrix products, arithmetic and copies ran while one was open for 20% -> 19% of each run, Pallas kernels for 0% -> 0%
where the time goes in v1:
time: 1030 us; the launch traced here: 1020 us
  waiting for transfers between devices  721 us (70%)
  matrix products  146 us (14%)
  local copies, waits for them, and re-layouts  57.3 us (6%)
  other arithmetic  56.8 us (6%)
  starting transfers between devices  16 us (2%)
  between operations  15.3 us (1%)
    reduce_scatter x1, waiting for transfers between devices, body(): lax.psum_scatter(grad_up, 'fsdp', scatter_dimension=0, tiled=True)  165 us
    reduce_scatter x1, waiting for transfers between devices, body(): lax.psum_scatter(grad_down, 'fsdp', scatter_dimension=0, tiled=True)  165 us
    reduce_scatter x1, waiting for transfers between devices, body(): lax.psum_scatter(grad_attn, 'fsdp', scatter_dimension=0, tiled=True)  80.8 us
    all_gather x1, waiting for transfers between devices, body(): lax.all_gather(low_up, 'fsdp', axis=0, tiled=True)  75.4 us
    psum x1, waiting for transfers between devices, body(): lax.psum((sum_attn, sum_proj, sum_up, sum_down, sum_vec), 'dp')  69.2 us
    all_gather x1, waiting for transfers between devices, body(): lax.all_gather(low_down, 'fsdp', axis=0, tiled=True)  64.4 us
    unnamed x11, waiting for transfers between devices  59.9 us
    dot_general x4, matrix products, contract_cols(): lax.dot_general(left, right, (((1,), (1,)), ((), ())), preferred_element_...  33.4 us
  transfers between devices with their start and end apart: 17, of which 13 were waited for; matrix products, arithmetic and copies ran while one was open for 19% of the time, Pallas kernels for 0%

profile of v1, /device:TPU:0, one launch (start us, length us, event | category | flops | bytes accessed | tf_op | source)
XLA Modules:
  0.0 1019.2 jit_solution(11269909110236448289)
XLA Ops:
  45.4 33.0 %all-gather.5.cloned.1.call-done = bf16[768,2304]{1,0:T(8,128)(2,1)} async-done(((bf16[96,2304]{1,0:T(8,128)(2,1)}), bf16[768,2304]{1,0:T(8,128)(2,1)}) %all-gather.5.cloned.1.call-update) | async-done | bytes 3538960 | tf_op jit(solution)/shard_map/all_gather | solution.py:152
  78.4 7.8 add_convert_fusion
  92.8 27.6 %while.22 = (s32[]{:T(128)}, bf16[2,512,768]{2,1,0:T(8,128)(2,1)}, f32[2,12,512]{2,1,0:T(8,128)S(1)}, bf16[2,512,2304]{1,2,0:T(8,128)(2,1)}, s32[2,512]{1,0:T(2,128)S(1)}, /*index=5*/s32[]{:T(128)}) while((s32[]{:T(128)}, bf16[2,512,768]{2,1,0:T(8,128)(2,1)}, f32[2,12,512]{2,1,0:T(8,128)S(1)}, bf16[2,512,2304]{1,2,0:T(8,128)(2,1)}, ...), condition=%wide.region_5.6_spmd, body=%wide.region_2.5_spmd.sunk | while | flops 843704320 | bytes 54753372 | solution.py:177
  126.5 75.4 %all-gather.9.cloned.1.call-done = bf16[768,3072]{1,0:T(8,128)(2,1)} async-done(((bf16[96,3072]{1,0:T(8,128)(2,1)}), bf16[768,3072]{1,0:T(8,128)(2,1)}) %all-gather.9.cloned.1.call-update) | async-done | bytes 4718608 | tf_op jit(solution)/shard_map/all_gather | solution.py:154
  201.9 15.9 %multiply_convert_fusion.3 = (bf16[1024,3072]{1,0:T(8,128)(2,1)}, f32[1024,3072]{1,0:T(8,128)}) fusion(f32[3072]{0:T(1024)S(1)} %copy-done.46, bf16[768,3072]{1,0:T(8,128)(2,1)} %all-gather.9.cloned.1.call-done, f32[1024,768]{0,1:T(8,128)} %copy-done.7, f32[768]{0:T(1024)S(1)} %copy-done.49, f32[768]{0:T(1024)S(1)} %copy-done.40, f32[1024]{0:T(1024)S(1)} %fusion.42, ...), kind=kOutput, calls=%fused_computation.41 | convolution fusion | flops 4867227648 | bytes 26765312 | tf_op jit(solution)/shard_map/dot_general | solution.py:183
  217.8 64.4 %all-gather.11.cloned.1.call-done = bf16[3072,768]{1,0:T(8,128)(2,1)} async-done(((bf16[384,768]{1,0:T(8,128)(2,1)}), bf16[3072,768]{1,0:T(8,128)(2,1)}) %all-gather.11.cloned.1.call-update) | async-done | bytes 4718608 | tf_op jit(solution)/shard_map/all_gather | solution.py:155
  282.2 15.5 %convert_reduce_fusion = (f32[3072]{0:T(1024)}, bf16[1024,3072]{1,0:T(8,128)(2,1)S(1)}) fusion(f32[1024,3072]{1,0:T(8,128)} %get-tuple-element.239, f32[3072]{0:T(1024)S(1)} %copy-done.46, bf16[1024,768]{1,0:T(8,128)(2,1)S(1)} %copy-done.15, bf16[3072,768]{1,0:T(8,128)(2,1)} %all-gather.11.cloned.1.call-done), kind=kOutput, calls=%fused_computation.40 | convolution fusion | flops 4904186880 | bytes 25190400 | tf_op jit(solution)/shard_map/dot_general | solution.py:52
  297.7 7.3 fusion.61
  312.3 10.5 %fusion.54 = (f32[1024]{0:T(1024)S(1)}, f32[1024,768]{0,1:T(8,128)S(1)}, bf16[1024,768]{0,1:T(8,128)(2,1)}) fusion(f32[1024]{0:T(1024)S(1)} %multiply_multiply_fusion.8, f32[1024,768]{0,1:T(8,128)S(1)} %copy-done.8, f32[1024]{0:T(1024)S(1)} %broadcast_multiply_fusion, f32[1024]{0:T(1024)S(1)} %fusion.42, f32[1024,768]{0,1:T(8,128)S(1)} %copy-done.10, ...), kind=kOutput, calls=%fused_computation.116 | convolution fusion | flops 4839701504 | bytes 22042624 | tf_op jit(solution)/shard_map/dot_general | solution.py:186
  331.0 52.6 %while.23 = (s32[]{:T(128)}, bf16[2,512,2304]{1,2,0:T(8,128)(2,1)}, bf16[2,512,2304]{1,2,0:T(8,128)(2,1)}, s32[2,512]{1,0:T(2,128)S(1)}, f32[2,12,512]{2,1,0:T(8...) while((s32[]{:T(128)}, bf16[2,512,2304]{1,2,0:T(8,128)(2,1)}, bf16[2,512,2304]{1,2,0:T(8,128)(2,1)}, ...), condition=%wide.region_12.13_spmd, body=%wide.region_10.12_spmd.sunk | while | flops 2069751808 | bytes 120764512 | solution.py:214
  338.6 6.9 multiply_reduce_fusion.5
  345.5 7.1 multiply_convert_fusion.7
  364.9 6.9 multiply_reduce_fusion.5
  371.8 7.0 multiply_convert_fusion.7
  383.5 6.9 copy.81
  390.5 8.7 fusion.43
  399.8 10.7 %fusion.46 = f32[768,3072]{1,0:T(8,128)} fusion(bf16[1024,3072]{1,0:T(8,128)(2,1)} %copy-done.59, f32[1024,768]{0,1:T(8,128)} %copy-done.7, f32[768]{0:T(1024)S(1)} %copy-done.50, f32[768]{0:T(1024)S(1)} %copy-done.41, f32[1024]{0:T(1024)S(1)} %copy-done.44, f32[1024]{0:T(1024)S(1)} %copy-done.36), kind=kOutput, calls=%fused_computation.114 | convolution fusion | flops 4835770368 | bytes 18888704 | tf_op jit(solution)/shard_map/dot_general | solution.py:46
  412.0 10.2 %fusion.64 = f32[3072,768]{1,0:T(8,128)} fusion(bf16[1024,3072]{1,0:T(8,128)(2,1)} %get-tuple-element.238, bf16[1024,768]{1,0:T(8,128)(2,1)S(1)} %copy-done.16), kind=kOutput, calls=%fused_computation.125 | convolution fusion | flops 4831838208 | bytes 17301504 | tf_op jit(solution)/shard_map/dot_general | solution.py:46
  426.4 7.9 fusion.60
  447.6 80.8 %reduce-scatter.8.cloned.1.call-done = f32[96,2304]{1,0:T(8,128)} async-done(((f32[768,2304]{1,0:T(8,128)}), f32[96,2304]{1,0:T(8,128)}) %reduce-scatter.8.cloned.1.call-update) | async-done | bytes 884752 | tf_op jit(solution)/shard_map/reduce_scatter | solution.py:239
  528.4 164.9 %reduce-scatter.12.cloned.1.call-done = f32[96,3072]{1,0:T(8,128)} async-done(((f32[768,3072]{1,0:T(8,128)}), f32[96,3072]{1,0:T(8,128)}) %reduce-scatter.12.cloned.1.call-update) | async-done | bytes 1179664 | tf_op jit(solution)/shard_map/reduce_scatter | solution.py:207
  693.2 164.8 %reduce-scatter.14.cloned.1.call-done = f32[384,768]{1,0:T(8,128)} async-done(((f32[3072,768]{1,0:T(8,128)}), f32[384,768]{1,0:T(8,128)}) %reduce-scatter.14.cloned.1.call-update) | async-done | bytes 1179664 | tf_op jit(solution)/shard_map/reduce_scatter | solution.py:208
  863.4 59.8 %reduce-scatter.16.cloned.1.call-done = f32[96,12]{1,0:T(8,128)} async-done(((f32[768,12]{1,0:T(8,128)}), f32[96,12]{1,0:T(8,128)}) %reduce-scatter.16.cloned.1.call-update) | async-done | bytes 4624
  930.5 69.2 %all-reduce.3.cloned.1.call-done = (f32[96,2304]{1,0:T(8,128)}, f32[96,768]{1,0:T(8,128)}, f32[96,3072]{1,0:T(8,128)}, f32[384,768]{1,0:T(8,128)}) async-done(((f32[96,2304]{1,0:T(8,128)}, f32[96,768]{1,0:T(8,128)}, f32[96,3072]{1,0:T(8,128)}, f32[384,768]{1,0:T(8,128)}), (f32[96,2304]{1,0:T(8,128)}, f32[96,768]{1,0:T(8,128)}, f32[96,3072]{1,0:T(8,128)}, f32[384,768]{1,0:T(8,128)})) %all-reduce.3.cloned.1.call-update) | async-done | bytes 3538960 | tf_op jit(solution)/shard_map/psum | solution.py:243
  (269 shorter events, 162.2 us)
Async XLA Ops:
  7.2 71.1 %all-gather.5.cloned.1.call-start = ((), (), s32[]{:S(2)}) async-start(), calls=%async_computation.5 | async-start | bytes 3981312 | tf_op jit(solution)/shard_map/all_gather | solution.py:152
  9.4 111.6 %all-gather.7.cloned.1.call-start = ((), (), s32[]{:S(2)}) async-start(), calls=%async_computation.6 | async-start | bytes 1327104 | tf_op jit(solution)/shard_map/all_gather | solution.py:153
  11.1 190.7 %all-gather.9.cloned.1.call-start = ((), (), s32[]{:S(2)}) async-start(), calls=%async_computation.7 | async-start | bytes 5308416 | tf_op jit(solution)/shard_map/all_gather | solution.py:154
  12.1 270.1 %all-gather.11.cloned.1.call-start = ((), (), s32[]{:S(2)}) async-start(), calls=%async_computation.8 | async-start | bytes 5308416 | tf_op jit(solution)/shard_map/all_gather | solution.py:155
  12.2 12.5 %collective-permute-start.1 = (bf16[96,12]{0,1:T(8,128)(2,1)S(1)}, bf16[96,12]{0,1:T(8,128)(2,1)S(1)}, u32[]{:S(2)}, u32[]{:S(2)}) collective-permute-start(bf16[96,12]{0,1:T(8,128)(2,1)S(1)} %convert_element_type.92), channel_id=1, source_target_pairs={{0,7},{1,0},{2,1},{3,2},{4,3},{5,4},{6,5},{7,6},{8,15},{9,8},{10,9... | collective-permute-start | bytes 6920 | tf_op jit(solution)/shard_map/ppermute | solution.py:31
  18.2 6.4 collective-permute-start
  19.1 428.5 %reduce-scatter.10.cloned.1.call-start = ((), (), s32[]{:S(2)}) async-start(), calls=%async_computation.10 | async-start | bytes 2654208 | tf_op jit(solution)/shard_map/reduce_scatter | solution.py:240
  20.9 100.1 %copy-start = (bf16[1024,768]{0,1:T(8,128)(2,1)}, bf16[1024,768]{0,1:T(8,128)(2,1)S(1)}, u32[]{:S(2)}) copy-start(bf16[1024,768]{0,1:T(8,128)(2,1)S(1)} %copy.73) | copy-start | bytes 4718596
  24.6 6.5 collective-permute-start.2
  24.6 6.5 collective-permute-start.3
  31.2 6.5 collective-permute-start.4
  31.2 10.6 %collective-permute-start.5 = (bf16[96,12]{0,1:T(8,128)(2,1)S(1)}, bf16[96,12]{0,1:T(8,128)(2,1)S(1)}, u32[]{:S(2)}, u32[]{:S(2)}) collective-permute-start(bf16[96,12]{0,1:T(8,128)(2,1)S(1)} %collective-permute-done.3), channel_id=1, source_target_pairs={{0,7},{1,0},{2,1},{3,2},{4,3},{5,4},{6,5},{7,6},{8,15},{9,8},{10,9... | collective-permute-start | bytes 6920 | tf_op jit(solution)/shard_map/ppermute | solution.py:31
  37.7 6.3 collective-permute-start.6
  124.4 77.4 %copy-start.40 = (f32[768]{0:T(1024)S(1)}, f32[768]{0:T(1024)}, u32[]{:S(2)}) copy-start(f32[768]{0:T(1024)} %get-tuple-element.170) | copy-start | bytes 9220
  124.4 77.4 %copy-start.46 = (f32[3072]{0:T(1024)S(1)}, f32[3072]{0:T(1024)}, u32[]{:S(2)}) copy-start(f32[3072]{0:T(1024)} %add.308) | copy-start | bytes 36868
  124.5 187.7 %copy-start.35 = (f32[1024]{0:T(1024)}, f32[1024]{0:T(1024)S(1)}, u32[]{:S(2)}) copy-start(f32[1024]{0:T(1024)S(1)} %broadcast_multiply_fusion) | copy-start | bytes 12292
  126.5 185.7 %copy-start.43 = (f32[1024]{0:T(1024)}, f32[1024]{0:T(1024)S(1)}, u32[]{:S(2)}) copy-start(f32[1024]{0:T(1024)S(1)} %fusion.42) | copy-start | bytes 12292
  201.9 80.3 %copy-start.15 = (bf16[1024,768]{1,0:T(8,128)(2,1)S(1)}, bf16[1024,768]{1,0:T(8,128)(2,1)}, u32[]{:S(2)}) copy-start(bf16[1024,768]{1,0:T(8,128)(2,1)} %param.23) | copy-start | bytes 4718596
  328.2 200.2 %reduce-scatter.8.cloned.1.call-start = ((), (), s32[]{:S(2)}) async-start(), calls=%async_computation.9 | async-start | bytes 7962624 | tf_op jit(solution)/shard_map/reduce_scatter | solution.py:239
  399.2 294.1 %reduce-scatter.12.cloned.1.call-start = ((), (), s32[]{:S(2)}) async-start(), calls=%async_computation.11 | async-start | bytes 10616832 | tf_op jit(solution)/shard_map/reduce_scatter | solution.py:207
  410.6 447.4 %reduce-scatter.14.cloned.1.call-start = ((), (), s32[]{:S(2)}) async-start(), calls=%async_computation.12 | async-start | bytes 10616832 | tf_op jit(solution)/shard_map/reduce_scatter | solution.py:208
  422.2 501.0 %reduce-scatter.16.cloned.1.call-start = ((), (), s32[]{:S(2)}) async-start(), calls=%async_computation.13 | async-start | bytes 442368
  447.5 552.1 %all-reduce.3.cloned.1.call-start = ((), (), s32[]{:S(2)}) async-start(), calls=%async_computation.14 | async-start | bytes 7077888 | tf_op jit(solution)/shard_map/psum | solution.py:243
  861.1 138.6 %copy-start.17 = (f32[96,768]{1,0:T(8,128)S(1)}, f32[96,768]{1,0:T(8,128)}, u32[]{:S(2)}) copy-start(f32[96,768]{1,0:T(8,128)} %param.28) | copy-start | bytes 884740
  (53 other events, 709.9 us)
Sparse Core Ops, SparseCore 0:
  10.8 67.5 all-gather.4
  81.1 39.8 all-gather.6
  123.8 78.0 all-gather.8
  204.5 77.6 all-gather.10
  328.3 68.0 reduce-scatter.9
  400.0 128.3 reduce-scatter.7
  532.0 161.2 reduce-scatter.11
  696.8 161.1 reduce-scatter.13
  861.9 61.2 reduce-scatter.15
  925.7 73.9 all-reduce.2
